TPU v7x, 32 devices: a whole 2x2x4 slice. The times are simulated.
32 devices in a mesh: dp: 8 (over z, y), tensor: 4 (over x, core).
Axes of the slice: x: 2, y: 2, z: 4, core: 2. Of those that a mesh axis runs over, the one named last changes fastest.
Arguments:
- tokens: bfloat16 [16384, 768], P('dp'), may hold values from -8 to 8
- lengths: int32 [8, 16], P('dp'), may hold values from 1 to 1024, 2048 in all within a row
- attn_gain: float32 [768], replicated, may hold values from 0.1 to 1.9
- qkv_weight: bfloat16 [768, 3, 768], P('dp', None, 'tensor'), may hold values from -0.21875 to 0.21875
- out_weight: bfloat16 [768, 768], P('tensor', 'dp'), may hold values from -0.625 to 0.625
- mlp_gain: float32 [768], replicated, may hold values from 0.1 to 1.9
- up_weight: bfloat16 [768, 2, 1152], P('dp', None, 'tensor'), may hold values from -0.21875 to 0.21875
- down_weight: bfloat16 [1152, 768], P('tensor', 'dp'), may hold values from -0.25 to 0.25
- cotangent: bfloat16 [16384, 768], P('dp'), may hold values from -8 to 8
Outputs:
- output: bfloat16 [16384, 768], P('dp')
- tokens_grad: float32 [16384, 768], P('dp')
- attn_gain_grad: float32 [768], P('dp')
- qkv_grad: float32 [768, 3, 768], P('dp', None, 'tensor')
- out_grad: float32 [768, 768], P('tensor', 'dp')
- mlp_gain_grad: float32 [768], P('dp')
- up_grad: float32 [768, 2, 1152], P('dp', None, 'tensor')
- down_grad: float32 [1152, 768], P('tensor', 'dp')
Inputs may be any that keep to these rules, and one draw needn't show every extreme that they name: Each row's 16 document lengths sum to 2048, and the longest of every row is exactly 1024.
All inputs are finite; a program needn't handle non-finite values.
Results may differ from a plain program's by a relative error of at most 0.02.
Values may be sent and summed in bfloat16 or wider, within the bound.
No kernel may reach another device: no remote copies, remote signals or barrier semaphores. Data moves between devices by JAX's collectives and lax.ppermute only.
A program may use at most 192 MiB of HBM per device.

v0:
```python
import math

import jax
import jax.numpy as jnp
from jax import lax
from jax.sharding import PartitionSpec as P

HD = 64
BLOCK = 512


eps_norm = 1e-05
theta_base = 160000.0


def cut_along(value, dim, count):
    shape = value.shape
    pieces = value.reshape(*shape[:dim], count, shape[dim] // count, *shape[dim + 1 :])
    return jnp.moveaxis(pieces, dim, 0)


def sent_and_summed(value, axis, dim):
    pieces = cut_along(value, dim, lax.axis_size(axis))
    arrived = lax.all_to_all(pieces, axis, split_axis=0, concat_axis=0, tiled=True)
    return arrived.astype(jnp.float32).sum(axis=0)


def in_one_piece(arrays, axis, dim, along):
    widths = [math.prod(a.shape[along:]) for a in arrays]
    both = jnp.concatenate(
        [a.reshape(*a.shape[:along], w) for a, w in zip(arrays, widths)], axis=along
    )
    result = sent_and_summed(both, axis, dim)
    pieces = jnp.split(result, [sum(widths[:k]) for k in range(1, len(widths))], axis=along)
    return tuple(
        (b.reshape(*result.shape[:along], *a.shape[along:]) for a, b in zip(arrays, pieces))
    )


def in_one_piece_2(arrays, axis, dim, along):
    widths = [a.shape[along] for a in arrays]
    both = jnp.concatenate(arrays, axis=along)
    result = sent_and_summed(both, axis, dim)
    return tuple(jnp.split(result, [sum(widths[:k]) for k in range(1, len(widths))], axis=along))


def row_layout(row_lengths, tok_count):
    doc_ends = jnp.cumsum(row_lengths, dtype=jnp.int32)
    tok_place = jnp.arange(tok_count, dtype=jnp.int32)
    passed = tok_place[:, None] >= doc_ends[None, :]
    segment = jnp.sum(passed.astype(jnp.int32), axis=1, dtype=jnp.int32)
    doc_start = jnp.sum(jnp.where(passed, row_lengths[None, :], 0), axis=1, dtype=jnp.int32)
    return (segment, tok_place - doc_start)


def rotary_tables(position, head_width):
    half_width = head_width // 2
    freq_index = jnp.arange(half_width, dtype=jnp.float32)
    inv_freq = jnp.exp(freq_index * (-2.0 * math.log(theta_base) / head_width))
    angles = position.astype(jnp.float32)[:, None] * inv_freq[None, :]
    angles = jnp.concatenate([angles, angles], axis=1)
    return (jnp.cos(angles), jnp.sin(angles))


def rotate(vector, cosine, sine_table):
    half_width = vector.shape[-1] // 2
    turned = jnp.concatenate([-vector[..., half_width:], vector[..., :half_width]], axis=-1)
    return vector * cosine[:, None, :] + turned * sine_table[:, None, :]


def rotate_back(upstream, cosine, sine_table):
    half_width = upstream.shape[-1] // 2
    moved = upstream * sine_table[:, None, :]
    turned = jnp.concatenate([moved[..., half_width:], -moved[..., :half_width]], axis=-1)
    return upstream * cosine[:, None, :] + turned


def normalize(vector):
    row_mean = jnp.mean(vector, axis=-1, keepdims=True)
    centred = vector - row_mean
    spread = jnp.mean(centred * centred, axis=-1, keepdims=True)
    factor = lax.rsqrt(spread + eps_norm)
    return (centred * factor, factor)


def norm_back(grad_norm_out, normed, factor, gain_vec):
    grad_normed = grad_norm_out * gain_vec
    first_mean = jnp.mean(grad_normed, axis=-1, keepdims=True)
    second_mean = jnp.mean(grad_normed * normed, axis=-1, keepdims=True)
    return factor * (grad_normed - first_mean - normed * second_mean)


def exact_gelu(vector):
    return jax.nn.gelu(vector, approximate=False)


def masked_scores(query_block, seg_block, key_rows, segment, score_scale):
    scores = (
        jnp.einsum("qhd,khd->hqk", query_block, key_rows, preferred_element_type=jnp.float32)
        * score_scale
    )
    same_doc = (seg_block[:, None] == segment[None, :])[None]
    return jnp.where(same_doc, scores, -1e30)


def attend_rows(query_block, seg_block, key_rows, value_rows, segment, score_scale):
    masked = masked_scores(query_block, seg_block, key_rows, segment, score_scale)
    row_max = jnp.max(masked, axis=2, keepdims=True)
    expos = jnp.exp(masked - row_max)
    row_sum = jnp.sum(expos, axis=2, keepdims=True)
    probs_low = (expos / row_sum).astype(jnp.bfloat16)
    attended = jnp.einsum("hqk,khd->qhd", probs_low, value_rows, preferred_element_type=jnp.float32)
    return (attended, row_max[..., 0] + jnp.log(row_sum[..., 0]))


def attend_back(
    query_block, seg_block, grad_block, log_total, key_rows, value_rows, segment, score_scale
):
    masked = masked_scores(query_block, seg_block, key_rows, segment, score_scale)
    probabilities = jnp.exp(masked - log_total[..., None])
    probs_low = probabilities.astype(jnp.bfloat16)
    grad_probs = jnp.einsum(
        "qhd,khd->hqk", grad_block, value_rows, preferred_element_type=jnp.float32
    )
    inner_sum = jnp.sum(probabilities * grad_probs, axis=2, keepdims=True)
    grad_scores = (probabilities * (grad_probs - inner_sum)).astype(jnp.bfloat16)
    grad_query = (
        jnp.einsum("hqk,khd->qhd", grad_scores, key_rows, preferred_element_type=jnp.float32)
        * score_scale
    )
    grad_keys = (
        jnp.einsum("hqk,qhd->khd", grad_scores, query_block, preferred_element_type=jnp.float32)
        * score_scale
    )
    grad_values = jnp.einsum(
        "hqk,qhd->khd", probs_low, grad_block, preferred_element_type=jnp.float32
    )
    return (grad_query, grad_keys, grad_values)


def shards(
    tokens, lengths, attn_gain, qkv_weight, out_weight, mlp_gain, up_weight, down_weight, cotangent
):
    tok_count = tokens.shape[0]
    qkv_full, up_full = (
        lax.all_gather(qkv_weight, "dp", axis=0, tiled=True),
        lax.all_gather(up_weight, "dp", axis=0, tiled=True),
    )
    out_full, down_full = (
        lax.all_gather(out_weight, "dp", axis=1, tiled=True),
        lax.all_gather(down_weight, "dp", axis=1, tiled=True),
    )
    head_cols = qkv_full.shape[2]
    heads_dev = head_cols // HD
    score_scale = HD ** (-0.5)
    block_count = tok_count // BLOCK
    segment, position = row_layout(lengths[0], tok_count)
    cosine, sine_table = rotary_tables(position, HD)
    source = tokens.astype(jnp.float32)
    normed_one, factor_one = normalize(source)
    h_one = (normed_one * attn_gain).astype(jnp.bfloat16)
    qkv_rows = jnp.einsum("td,dcf->tcf", h_one, qkv_full, preferred_element_type=jnp.float32)
    queries = rotate(qkv_rows[:, 0].reshape(tok_count, heads_dev, HD), cosine, sine_table).astype(
        jnp.bfloat16
    )
    key_rows = rotate(qkv_rows[:, 1].reshape(tok_count, heads_dev, HD), cosine, sine_table).astype(
        jnp.bfloat16
    )
    value_rows = qkv_rows[:, 2].reshape(tok_count, heads_dev, HD).astype(jnp.bfloat16)
    query_blocks = queries.reshape(block_count, BLOCK, heads_dev, HD)
    seg_blocks = segment.reshape(block_count, BLOCK)

    def forward_block(block_item):
        return attend_rows(block_item[0], block_item[1], key_rows, value_rows, segment, score_scale)

    attended, log_totals = lax.map(forward_block, (query_blocks, seg_blocks))
    attended = attended.reshape(tok_count, head_cols).astype(jnp.bfloat16)
    attn_part = jnp.dot(attended, out_full, preferred_element_type=jnp.float32)
    mid = source + lax.psum(attn_part.astype(jnp.bfloat16), "tensor").astype(jnp.float32)
    normed_two, factor_two = normalize(mid)
    h_two = (normed_two * mlp_gain).astype(jnp.bfloat16)
    gate_up = jnp.einsum("td,dcf->tcf", h_two, up_full, preferred_element_type=jnp.float32)
    active, gelu_pull = jax.vjp(exact_gelu, gate_up[:, 0])
    hidden = (active * gate_up[:, 1]).astype(jnp.bfloat16)
    mlp_part = jnp.dot(hidden, down_full, preferred_element_type=jnp.float32)
    output = (mid + lax.psum(mlp_part.astype(jnp.bfloat16), "tensor").astype(jnp.float32)).astype(
        jnp.bfloat16
    )
    held_back = lax.optimization_barrier((qkv_weight, up_weight, out_weight, down_weight, output))
    qkv_back, up_back = (
        lax.all_gather(held_back[0], "dp", axis=0, tiled=True),
        lax.all_gather(held_back[1], "dp", axis=0, tiled=True),
    )
    out_back, down_back = (
        lax.all_gather(held_back[2], "dp", axis=1, tiled=True),
        lax.all_gather(held_back[3], "dp", axis=1, tiled=True),
    )
    grad_down_weight = jnp.einsum(
        "tf,td->fd", hidden, cotangent, preferred_element_type=jnp.float32
    )
    grad_hidden = jnp.einsum(
        "td,fd->tf", cotangent, down_back, preferred_element_type=jnp.float32
    ).astype(jnp.bfloat16)
    grad_wide = grad_hidden.astype(jnp.float32)
    (grad_gate,) = gelu_pull(grad_wide * gate_up[:, 1])
    grad_gate_up = jnp.stack([grad_gate, grad_wide * active], axis=1).astype(jnp.bfloat16)
    grad_up_weight = jnp.einsum(
        "td,tcf->dcf", h_two, grad_gate_up, preferred_element_type=jnp.float32
    )
    grad_h_two = lax.psum(
        jnp.einsum("tcf,dcf->td", grad_gate_up, up_back, preferred_element_type=jnp.float32).astype(
            jnp.bfloat16
        ),
        "tensor",
    ).astype(jnp.float32)
    grad_mlp_gain = jnp.sum(grad_h_two * normed_two, axis=0)
    grad_mid = cotangent.astype(jnp.float32) + norm_back(
        grad_h_two, normed_two, factor_two, mlp_gain
    )
    grad_mid_low = grad_mid.astype(jnp.bfloat16)
    grad_out_weight = jnp.einsum(
        "tf,td->fd", attended, grad_mid_low, preferred_element_type=jnp.float32
    )
    grad_attended = jnp.einsum(
        "td,fd->tf", grad_mid_low, out_back, preferred_element_type=jnp.float32
    ).astype(jnp.bfloat16)
    grad_blocks = grad_attended.reshape(block_count, BLOCK, heads_dev, HD)
    zeros_kd = jnp.zeros((tok_count, heads_dev, HD), jnp.float32)

    def backward_block(carried, block_item):
        grad_query, grad_keys, grad_values = attend_back(
            block_item[0],
            block_item[1],
            block_item[2],
            block_item[3],
            key_rows,
            value_rows,
            segment,
            score_scale,
        )
        return ((carried[0] + grad_keys, carried[1] + grad_values), grad_query)

    (grad_keys, grad_values), grad_query = lax.scan(
        backward_block, (zeros_kd, zeros_kd), (query_blocks, seg_blocks, grad_blocks, log_totals)
    )
    grad_query = rotate_back(grad_query.reshape(tok_count, heads_dev, HD), cosine, sine_table)
    grad_keys = rotate_back(grad_keys, cosine, sine_table)
    grad_qkv = jnp.stack(
        [
            grad_query.reshape(tok_count, head_cols),
            grad_keys.reshape(tok_count, head_cols),
            grad_values.reshape(tok_count, head_cols),
        ],
        axis=1,
    ).astype(jnp.bfloat16)
    grad_qkv_weight = jnp.einsum("td,tcf->dcf", h_one, grad_qkv, preferred_element_type=jnp.float32)
    grad_h_one = lax.psum(
        jnp.einsum("tcf,dcf->td", grad_qkv, qkv_back, preferred_element_type=jnp.float32).astype(
            jnp.bfloat16
        ),
        "tensor",
    ).astype(jnp.float32)
    grad_attn_gain = jnp.sum(grad_h_one * normed_one, axis=0)
    grad_tokens = grad_mid + norm_back(grad_h_one, normed_one, factor_one, attn_gain)
    rows_part = in_one_piece(
        (
            grad_qkv_weight.astype(jnp.bfloat16),
            grad_up_weight.astype(jnp.bfloat16),
            grad_attn_gain.astype(jnp.bfloat16),
            grad_mlp_gain.astype(jnp.bfloat16),
        ),
        "dp",
        0,
        1,
    )
    cols_part = in_one_piece_2(
        (grad_out_weight.astype(jnp.bfloat16), grad_down_weight.astype(jnp.bfloat16)), "dp", 1, 0
    )
    return (
        output,
        grad_tokens,
        rows_part[2],
        rows_part[0],
        cols_part[0],
        rows_part[3],
        rows_part[1],
        cols_part[1],
    )


def solution(mesh):
    in_specs = (
        P("dp", None),
        P("dp", None),
        P(),
        P("dp", None, "tensor"),
        P("tensor", "dp"),
        P(),
        P("dp", None, "tensor"),
        P("tensor", "dp"),
        P("dp", None),
    )
    out_specs = (
        P("dp", None),
        P("dp", None),
        P("dp"),
        P("dp", None, "tensor"),
        P("tensor", "dp"),
        P("dp"),
        P("dp", None, "tensor"),
        P("tensor", "dp"),
    )
    return jax.shard_map(shards, mesh=mesh, in_specs=in_specs, out_specs=out_specs, check_vma=False)
```

profile of v0, /device:TPU:0, one launch (start us, length us, event | category | flops | bytes accessed | tf_op | source)
XLA Modules:
  0.0 863.9 jit_solution(5316221057405745326)
XLA Ops:
  13.4 40.5 %all_gather.24 = bf16[768,3,192]{2,1,0:T(4,128)(2,1)} all-gather(bf16[96,3,192]{2,1,0:T(4,128)(2,1)S(1)} %copy.102), channel_id=1, replica_groups=mesh['dp'=8,'tensor'=4] {'dp'}, dimensions={0}, use_global_device_ids=true | all-gather | bytes 995328 | tf_op jit(solution)/shard_map/all_gather | solution.py:146
  62.6 31.1 %all_gather.25 = bf16[192,768]{0,1:T(8,128)(2,1)S(1)} all-gather(bf16[192,96]{0,1:T(8,128)(2,1)S(1)} %copy.106), channel_id=1, replica_groups=mesh['dp'=8,'tensor'=4] {'dp'}, dimensions={1}, use_global_device_ids=true | all-gather | bytes 331776 | tf_op jit(solution)/shard_map/all_gather | solution.py:150
  115.3 88.2 %while.27 = (s32[]{:T(128)}, bf16[4,512,3,64]{1,3,2,0:T(8,128)(2,1)}, f32[4,3,512]{2,1,0:T(4,128)}, s32[4,512]{1,0:T(4,128)S(1)}, s32[2048]{0:T(1024)S(1)}, /*in...) while((s32[]{:T(128)}, ...), condition=%wide.region_8.9_spmd, body=%wide.region_5.8_spmd.sunk | while | flops 844102144 | bytes 50466988 | solution.py:176
  115.9 6.8 fusion.162
  122.8 6.8 fusion.163
  129.6 6.7 fusion.164
  137.9 6.8 fusion.162
  144.8 6.8 fusion.163
  151.6 6.7 fusion.164
  159.9 6.8 fusion.162
  166.8 6.8 fusion.163
  173.6 6.7 fusion.164
  181.9 6.8 fusion.162
  188.8 6.8 fusion.163
  195.6 6.7 fusion.164
  210.6 33.7 %all_gather.27 = bf16[288,768]{0,1:T(8,128)(2,1)} all-gather(bf16[288,96]{0,1:T(8,128)(2,1)S(1)} %copy.108), channel_id=1, replica_groups=mesh['dp'=8,'tensor'=4] {'dp'}, dimensions={1}, use_global_device_ids=true | all-gather | bytes 497664 | tf_op jit(solution)/shard_map/all_gather | solution.py:151
  244.3 34.9 %all_gather.26 = bf16[768,2,288]{2,1,0:T(2,128)(2,1)} all-gather(bf16[96,2,288]{2,1,0:T(2,128)(2,1)S(1)} %copy-done.33), channel_id=1, replica_groups=mesh['dp'=8,'tensor'=4] {'dp'}, dimensions={0}, use_global_device_ids=true | all-gather | bytes 995328 | tf_op jit(solution)/shard_map/all_gather | solution.py:147
  297.2 68.3 %all-reduce.7.cloned.1.call-done = bf16[2048,768]{1,0:T(8,128)(2,1)} async-done(((bf16[2048,768]{1,0:T(8,128)(2,1)}), bf16[2048,768]{1,0:T(8,128)(2,1)}) %all-reduce.7.cloned.1.call-update) | async-done | bytes 3145744 | tf_op jit(solution)/shard_map/psum | solution.py:186
  371.3 31.9 %all_gather.28 = bf16[288,768]{0,1:T(8,128)(2,1)S(1)} all-gather(bf16[288,96]{0,1:T(8,128)(2,1)S(1)} %copy.109), channel_id=1, replica_groups=mesh['dp'=8,'tensor'=4] {'dp'}, dimensions={1}, use_global_device_ids=true | all-gather | bytes 497664 | tf_op jit(solution)/shard_map/all_gather | solution.py:196
  403.3 34.3 %all_gather.29 = bf16[768,2,288]{2,0,1:T(8,128)(2,1)S(1)} all-gather(bf16[96,2,288]{2,0,1:T(8,128)(2,1)S(1)} %copy.110), channel_id=1, replica_groups=mesh['dp'=8,'tensor'=4] {'dp'}, dimensions={0}, use_global_device_ids=true | all-gather | bytes 995328 | tf_op jit(solution)/shard_map/all_gather | solution.py:192
  454.2 31.4 %all_gather.30 = bf16[192,768]{0,1:T(8,128)(2,1)S(1)} all-gather(bf16[192,96]{0,1:T(8,128)(2,1)} %copy.111), channel_id=1, replica_groups=mesh['dp'=8,'tensor'=4] {'dp'}, dimensions={1}, use_global_device_ids=true | all-gather | bytes 331776 | tf_op jit(solution)/shard_map/all_gather | solution.py:195
  485.6 35.4 %all_gather.31 = bf16[768,3,192]{2,0,1:T(8,128)(2,1)} all-gather(bf16[96,3,192]{2,0,1:T(8,128)(2,1)} %param.16), channel_id=1, replica_groups=mesh['dp'=8,'tensor'=4] {'dp'}, dimensions={0}, use_global_device_ids=true | all-gather | bytes 995328 | tf_op jit(solution)/shard_map/all_gather | solution.py:191
  521.0 7.0 fusion.59
  536.9 164.7 %while.28 = (s32[]{:T(128)}, f32[2048,3,64]{0,2,1:T(8,128)}, f32[2048,3,64]{0,2,1:T(8,128)}, f32[4,512,3,64]{1,0,3,2:T(4,128)}, bf16[4,512,3,64]{1,3,2,0:T(8,128...) while((s32[]{:T(128)}, f32[2048,3,64]{0,2,1:T(8,128)}, ...), condition=%wide.region_18.19_spmd.clone, body=%wide.region_16.18_spmd.clone.sunk | while | flops 2063563264 | bytes 142532864 | solution.py:243
  568.6 8.6 dynamic_update_slice.19
  610.0 8.6 dynamic_update_slice.19
  623.7 6.3 fusion.176
  651.4 8.6 dynamic_update_slice.19
  692.8 8.6 dynamic_update_slice.19
  750.0 36.6 %all-reduce.11.cloned.1.call-done = bf16[2048,768]{1,0:T(8,128)(2,1)} async-done(((bf16[2048,768]{1,0:T(8,128)(2,1)}), bf16[2048,768]{1,0:T(8,128)(2,1)}) %all-reduce.11.cloned.1.call-update) | async-done | bytes 3145744 | tf_op jit(solution)/shard_map/psum | solution.py:257
  809.9 6.5 fusion.53
  816.4 35.9 %all-to-all-done = bf16[8,96,1154]{2,1,0:T(8,128)(2,1)} async-done(((bf16[8,96,1154]{2,1,0:T(8,128)(2,1)}), bf16[8,96,1154]{2,1,0:T(8,128)(2,1)}, u32[]{:S(2)}, u32[]{:S(2)}) %all-to-all-start) | async-done | bytes 1772576 | tf_op jit(solution)/shard_map/all_to_all | solution.py:24
  (307 shorter events, 298.4 us)
Async XLA Ops:
  7.2 272.0 %all-reduce.5.cloned.1.call-start = ((), (), s32[]{:S(2)}) async-start(), calls=%async_computation.2 | async-start | bytes 6291456 | tf_op jit(solution)/shard_map/psum | solution.py:179
  12.2 45.1 %copy-start.39 = (f32[2048]{0:T(1024)}, f32[2048]{0:T(1024)S(1)}, u32[]{:S(2)}) copy-start(f32[2048]{0:T(1024)S(1)} %broadcast_multiply_fusion.9) | copy-start | bytes 24580
  13.2 44.1 %copy-start.52 = (f32[768]{0:T(1024)S(1)}, f32[768]{0:T(1024)}, u32[]{:S(2)}) copy-start(f32[768]{0:T(1024)} %param.15) | copy-start | bytes 9220
  13.3 47.4 %copy-start.44 = (f32[2048]{0:T(1024)}, f32[2048]{0:T(1024)S(1)}, u32[]{:S(2)}) copy-start(f32[2048]{0:T(1024)S(1)} %add_rsqrt_fusion.1) | copy-start | bytes 24580
  122.8 6.8 copy-start.30
  144.8 6.8 copy-start.30
  166.8 6.8 copy-start.30
  188.8 6.8 copy-start.30
  203.5 6.1 copy-start.5
  203.5 6.1 copy-start.12
  203.5 6.1 copy-start.43
  209.6 34.7 %copy-start.33 = (bf16[96,2,288]{2,1,0:T(2,128)(2,1)S(1)}, bf16[96,2,288]{2,1,0:T(2,128)(2,1)}, u32[]{:S(2)}) copy-start(bf16[96,2,288]{2,1,0:T(2,128)(2,1)} %param.19) | copy-start | bytes 331780
  209.6 69.6 %copy-start.3 = (bf16[2048,768]{1,0:T(8,128)(2,1)S(1)}, bf16[2048,768]{1,0:T(8,128)(2,1)}, u32[]{:S(2)}) copy-start(bf16[2048,768]{1,0:T(8,128)(2,1)} %param.13) | copy-start | bytes 9437188
  209.7 155.9 %all-reduce.7.cloned.1.call-start = ((), (), s32[]{:S(2)}) async-start(), calls=%async_computation.3 | async-start | bytes 6291456 | tf_op jit(solution)/shard_map/psum | solution.py:186
  282.1 245.9 %copy-start.41 = (f32[2048]{0:T(1024)}, f32[2048]{0:T(1024)S(1)}, u32[]{:S(2)}) copy-start(f32[2048]{0:T(1024)S(1)} %broadcast_multiply_fusion.8) | copy-start | bytes 24580
  286.6 6.0 copy-start.20
  286.6 7.0 copy-start.32
  297.2 223.8 %all-reduce.9.cloned.1.call-start = ((), (), s32[]{:S(2)}) async-start(), calls=%async_computation.4 | async-start | bytes 6291456 | tf_op jit(solution)/shard_map/psum | solution.py:210
  449.3 337.3 %all-reduce.11.cloned.1.call-start = ((), (), s32[]{:S(2)}) async-start(), calls=%async_computation.5 | async-start | bytes 6291456 | tf_op jit(solution)/shard_map/psum | solution.py:257
  521.0 7.0 copy-start.10
  521.0 7.0 copy-start.13
  521.0 7.0 copy-start.26
  521.0 7.0 copy-start.47
  521.0 7.0 copy-start.50
  559.6 5.1 copy-start
  564.8 12.5 %copy-start.7 = (bf16[2048,3,64]{0,2,1:T(8,128)(2,1)S(1)}, bf16[2048,3,64]{0,2,1:T(8,128)(2,1)}, u32[]{:S(2)}) copy-start(bf16[2048,3,64]{0,2,1:T(8,128)(2,1)} %get-tuple-element.589) | copy-start | bytes 2359300 | tf_op jit(solution)/shard_map/while
  605.6 13.1 %copy-start.7 = (bf16[2048,3,64]{0,2,1:T(8,128)(2,1)S(1)}, bf16[2048,3,64]{0,2,1:T(8,128)(2,1)}, u32[]{:S(2)}) copy-start(bf16[2048,3,64]{0,2,1:T(8,128)(2,1)} %get-tuple-element.589) | copy-start | bytes 2359300 | tf_op jit(solution)/shard_map/while
  647.0 13.1 %copy-start.7 = (bf16[2048,3,64]{0,2,1:T(8,128)(2,1)S(1)}, bf16[2048,3,64]{0,2,1:T(8,128)(2,1)}, u32[]{:S(2)}) copy-start(bf16[2048,3,64]{0,2,1:T(8,128)(2,1)} %get-tuple-element.589) | copy-start | bytes 2359300 | tf_op jit(solution)/shard_map/while
  688.4 13.1 %copy-start.7 = (bf16[2048,3,64]{0,2,1:T(8,128)(2,1)S(1)}, bf16[2048,3,64]{0,2,1:T(8,128)(2,1)}, u32[]{:S(2)}) copy-start(bf16[2048,3,64]{0,2,1:T(8,128)(2,1)} %get-tuple-element.589) | copy-start | bytes 2359300 | tf_op jit(solution)/shard_map/while
  719.8 9.1 %copy-start.54 = (bf16[768]{0:T(1024)(128)(2,1)S(1)}, bf16[768]{0:T(1024)(128)(2,1)}, u32[]{:S(2)}) copy-start(bf16[768]{0:T(1024)(128)(2,1)} %get-tuple-element.305) | copy-start | bytes 4612
  736.1 65.4 %all-to-all-start.1 = ((bf16[8,480,96]{1,2,0:T(8,128)(2,1)}), bf16[8,480,96]{1,2,0:T(8,128)(2,1)}, u32[]{:S(2)}, u32[]{:S(2)}) async-start(bf16[8,480,96]{1,2,0:T(8,128)(2,1)} %bitcast.263), calls=%async_computation.1 | async-start | bytes 1572864 | tf_op jit(solution)/shard_map/all_to_all | solution.py:24
  801.5 50.8 %all-to-all-start = ((bf16[8,96,1154]{2,1,0:T(8,128)(2,1)}), bf16[8,96,1154]{2,1,0:T(8,128)(2,1)}, u32[]{:S(2)}, u32[]{:S(2)}) async-start(bf16[8,96,1154]{2,1,0:T(8,128)(2,1)} %copy.116), calls=%async_computation | async-start | bytes 3932160 | tf_op jit(solution)/shard_map/all_to_all | solution.py:24
  (47 other events, 112.0 us)
Sparse Core Ops, SparseCore 0:
  209.8 67.8 all-reduce.4
  297.3 68.2 all-reduce.6
  449.4 68.2 all-reduce.8
  718.0 68.5 all-reduce.10
where the time goes:
time: 871 us; the launch traced here: 864 us
  blocking collectives  273 us (31%)
  matrix products  194 us (22%)
  waiting for transfers between devices  141 us (16%)
  other arithmetic  131 us (15%)
  local copies, waits for them, and re-layouts  98.1 us (11%)
  between operations  15.1 us (2%)
  starting transfers between devices  11 us (1%)
    psum x1, waiting for transfers between devices, shards(): lax.psum(mlp_part.astype(jnp.bfloat16), 'tensor').astype(jnp.float32)  68.3 us
    all_gather x1, blocking collectives, shards(): lax.all_gather(qkv_weight, 'dp', axis=0, tiled=True)  40.5 us
    dot_general x8, matrix products, masked_scores(): jnp.einsum('qhd,khd->hqk', query_block, key_rows, preferred_element_type=...  39.3 us
    psum x1, waiting for transfers between devices, shards(): lax.psum(jnp.einsum('tcf,dcf->td', grad_qkv, qkv_back, preferred_element_...  36.6 us
    dynamic_update_slice x8, local copies, waits for them, and re-layouts, shards(): attended, log_totals = lax.map(forward_block, (query_blocks, seg_blocks))  36.1 us
    all_to_all x2, waiting for transfers between devices, sent_and_summed(): lax.all_to_all(pieces, axis, split_axis=0, concat_axis=0, tiled=True)  35.9 us
    all_gather x1, blocking collectives, shards(): lax.all_gather(held_back[0], 'dp', axis=0, tiled=True)  35.4 us
    all_gather x1, blocking collectives, shards(): lax.all_gather(up_weight, 'dp', axis=0, tiled=True)  34.9 us
  transfers between devices with their start and end apart: 6, of which 3 were waited for; matrix products, arithmetic and copies ran while one was open for 6% of the time, Pallas kernels for 0%

commit v1 on v0

v1 whole, which is shorter than its diff:
```python
import math

import jax
import jax.numpy as jnp
from jax import lax
from jax.experimental import pallas as pl
from jax.experimental.pallas import tpu as pltpu
from jax.sharding import PartitionSpec as P

HD = 64


eps_norm = 1e-05
theta_base = 160000.0


def cut_along(value, dim, count):
    shape = value.shape
    pieces = value.reshape(*shape[:dim], count, shape[dim] // count, *shape[dim + 1 :])
    return jnp.moveaxis(pieces, dim, 0)


def sent_and_summed(value, axis, dim):
    pieces = cut_along(value, dim, lax.axis_size(axis))
    arrived = lax.all_to_all(pieces, axis, split_axis=0, concat_axis=0, tiled=True)
    return arrived.astype(jnp.float32).sum(axis=0)


def in_one_piece(arrays, axis, dim, along):
    widths = [math.prod(a.shape[along:]) for a in arrays]
    both = jnp.concatenate(
        [a.reshape(*a.shape[:along], w) for a, w in zip(arrays, widths)], axis=along
    )
    result = sent_and_summed(both, axis, dim)
    pieces = jnp.split(result, [sum(widths[:k]) for k in range(1, len(widths))], axis=along)
    return tuple(
        (b.reshape(*result.shape[:along], *a.shape[along:]) for a, b in zip(arrays, pieces))
    )


def in_one_piece_2(arrays, axis, dim, along):
    widths = [a.shape[along] for a in arrays]
    both = jnp.concatenate(arrays, axis=along)
    result = sent_and_summed(both, axis, dim)
    return tuple(jnp.split(result, [sum(widths[:k]) for k in range(1, len(widths))], axis=along))


def row_layout(row_lengths, tok_count):
    doc_ends = jnp.cumsum(row_lengths, dtype=jnp.int32)
    tok_place = jnp.arange(tok_count, dtype=jnp.int32)
    passed = tok_place[:, None] >= doc_ends[None, :]
    segment = jnp.sum(passed.astype(jnp.int32), axis=1, dtype=jnp.int32)
    doc_start = jnp.sum(jnp.where(passed, row_lengths[None, :], 0), axis=1, dtype=jnp.int32)
    return (segment, tok_place - doc_start)


def tile_ranges(row_lengths, tok_count):
    ends = jnp.cumsum(row_lengths, dtype=jnp.int32)
    starts = ends - row_lengths
    begin = jnp.arange(tok_count // TILE, dtype=jnp.int32)[:, None] * TILE
    touched = (ends[None, :] > begin) & (starts[None, :] < begin + TILE)
    low = jnp.min(jnp.where(touched, starts[None, :], tok_count), axis=1)
    high = jnp.max(jnp.where(touched, ends[None, :], 0), axis=1)
    return (low // TILE, (high + TILE - 1) // TILE)


def rotary_tables(position, head_width):
    half_width = head_width // 2
    freq_index = jnp.arange(half_width, dtype=jnp.float32)
    inv_freq = jnp.exp(freq_index * (-2.0 * math.log(theta_base) / head_width))
    angles = position.astype(jnp.float32)[:, None] * inv_freq[None, :]
    cosine, sine = jnp.cos(angles), jnp.sin(angles)
    return (jnp.concatenate([cosine, cosine], axis=1), jnp.concatenate([-sine, sine], axis=1))


def normalize(vector):
    row_mean = jnp.mean(vector, axis=-1, keepdims=True)
    centred = vector - row_mean
    spread = jnp.mean(centred * centred, axis=-1, keepdims=True)
    factor = lax.rsqrt(spread + eps_norm)
    return (centred * factor, factor)


def norm_back(grad_norm_out, normed, factor, gain_vec):
    grad_normed = grad_norm_out * gain_vec
    first_mean = jnp.mean(grad_normed, axis=-1, keepdims=True)
    second_mean = jnp.mean(grad_normed * normed, axis=-1, keepdims=True)
    return factor * (grad_normed - first_mean - normed * second_mean)


def exact_gelu(vector):
    return jax.nn.gelu(vector, approximate=False)


TILE = 256
NEG = -1e30


def nt_dot(a, b):
    return lax.dot_general(a, b, (((1,), (1,)), ((), ())), preferred_element_type=jnp.float32)


def nn_dot(a, b):
    return lax.dot_general(a, b, (((1,), (0,)), ((), ())), preferred_element_type=jnp.float32)


def tn_dot(a, b):
    return lax.dot_general(a, b, (((0,), (0,)), ((), ())), preferred_element_type=jnp.float32)


def swap_halves(u):
    half = u.shape[-1] // 2
    return jnp.concatenate([u[:, half:], u[:, :half]], axis=1)


def twice(a):
    return jnp.concatenate([a, a], axis=1)


def lane_fold(op, a):
    return op(a[:, : TILE // 2], a[:, TILE // 2 :])


def whole(shape):
    return pl.BlockSpec(shape, lambda *_: (0,) * len(shape))


def project_heads(h_one, weight, cos_tab, sin_tab, heads):
    tok_count, width = h_one.shape
    cols = heads * HD
    rows = 2 * TILE

    def body(h_ref, w_ref, c_ref, s_ref, q_ref, k_ref, v_ref):
        full = nn_dot(h_ref[...], w_ref[...])
        cosine, sine = c_ref[...], s_ref[...]
        for h in range(heads):
            u = full[:, h * HD : (h + 1) * HD]
            turned = (u * cosine + swap_halves(u) * sine).astype(jnp.bfloat16)
            q_ref[h] = (turned.astype(jnp.float32) * HD**-0.5).astype(jnp.bfloat16)
            u = full[:, cols + h * HD : cols + (h + 1) * HD]
            k_ref[h] = (u * cosine + swap_halves(u) * sine).astype(jnp.bfloat16)
            v_ref[h] = full[:, 2 * cols + h * HD : 2 * cols + (h + 1) * HD].astype(jnp.bfloat16)

    out = jax.ShapeDtypeStruct((heads, tok_count, HD), jnp.bfloat16)
    return pl.pallas_call(
        body,
        grid=(tok_count // rows,),
        in_specs=[
            pl.BlockSpec((rows, width), lambda i: (i, 0)),
            whole(weight.shape),
            pl.BlockSpec((rows, HD), lambda i: (i, 0)),
            pl.BlockSpec((rows, HD), lambda i: (i, 0)),
        ],
        out_specs=[pl.BlockSpec((heads, rows, HD), lambda i: (0, i, 0))] * 3,
        out_shape=[out] * 3,
        name="project_heads",
    )(h_one, weight, cos_tab, sin_tab)


def attend(first, last, query, key, value, seg_col, seg_row):
    heads, tok_count, _ = query.shape
    blocks = tok_count // TILE
    half = TILE // 2

    def body(
        first_ref, last_ref, q_ref, k_ref, v_ref, col_ref, row_ref, low_ref, out_ref, lse_ref,
        scores, peak, total, accum,
    ):
        i = pl.program_id(0)
        lo, hi = first_ref[i], last_ref[i]
        peak[...] = jnp.full(peak.shape, NEG, jnp.float32)
        total[...] = jnp.zeros(total.shape, jnp.float32)
        accum[...] = jnp.zeros(accum.shape, jnp.float32)

        def score(j, carry):
            at = pl.multiple_of(j * TILE, TILE)
            same = twice(col_ref[...]) == row_ref[:, pl.ds(at, TILE)]
            for h in range(heads):
                s = jnp.where(same, nt_dot(q_ref[h], k_ref[h, pl.ds(at, TILE), :]), NEG)
                scores[h, j] = s
                peak[h] = jnp.maximum(peak[h], lane_fold(jnp.maximum, s))
            return carry

        lax.fori_loop(lo, hi, score, 0)
        for h in range(heads):
            peak[h] = jnp.broadcast_to(jnp.max(peak[h], axis=1, keepdims=True), (TILE, half))

        def spread(j, carry):
            at = pl.multiple_of(j * TILE, TILE)
            for h in range(heads):
                p = jnp.exp(scores[h, j] - twice(peak[h]))
                total[h] = total[h] + lane_fold(jnp.add, p)
                accum[h] = accum[h] + nn_dot(p.astype(jnp.bfloat16), v_ref[h, pl.ds(at, TILE), :])
            return carry

        lax.fori_loop(lo, hi, spread, 0)
        for h in range(heads):
            norm = jnp.sum(total[h], axis=1, keepdims=True)
            out = accum[h] / norm
            out_ref[h] = out
            low_ref[:, h * HD : (h + 1) * HD] = out.astype(jnp.bfloat16)
            logs = peak[h] + jnp.log(jnp.broadcast_to(norm, (TILE, half)))
            lse_ref[h] = jnp.transpose(logs)[0:1, :]

    tile = pl.BlockSpec((heads, TILE, HD), lambda i, *_: (0, i, 0))
    return pl.pallas_call(
        body,
        grid_spec=pltpu.PrefetchScalarGridSpec(
            num_scalar_prefetch=2,
            grid=(blocks,),
            in_specs=[
                tile,
                whole(key.shape),
                whole(value.shape),
                pl.BlockSpec((TILE, half), lambda i, *_: (i, 0)),
                whole(seg_row.shape),
            ],
            out_specs=[
                pl.BlockSpec((TILE, heads * HD), lambda i, *_: (i, 0)),
                tile,
                pl.BlockSpec((heads, 1, TILE), lambda i, *_: (0, 0, i)),
            ],
            scratch_shapes=[
                pltpu.VMEM((heads, blocks, TILE, TILE), jnp.float32),
                pltpu.VMEM((heads, TILE, half), jnp.float32),
                pltpu.VMEM((heads, TILE, half), jnp.float32),
                pltpu.VMEM((heads, TILE, HD), jnp.float32),
            ],
        ),
        out_shape=[
            jax.ShapeDtypeStruct((tok_count, heads * HD), jnp.bfloat16),
            jax.ShapeDtypeStruct((heads, tok_count, HD), jnp.float32),
            jax.ShapeDtypeStruct((heads, 1, tok_count), jnp.float32),
        ],
        name="attend",
    )(first, last, query, key, value, seg_col, seg_row)


def attend_grad(
    first, last, query, key, value, seg_col, seg_row, grad, out, lse, cos_tab, sin_tab
):
    heads, tok_count, _ = query.shape
    blocks = tok_count // TILE
    half = TILE // 2
    cols = heads * HD

    def body(
        first_ref, last_ref, q_ref, k_ref, v_ref, col_ref, row_ref, g_ref, o_ref, lse_ref,
        c_ref, s_ref, d_ref, split, inner, dq, dk, dv,
    ):
        j = pl.program_id(0)
        lo, hi = first_ref[j], last_ref[j]
        here = pl.ds(pl.multiple_of(j * TILE, TILE), TILE)

        @pl.when(j == 0)
        def _():
            dq[...] = jnp.zeros(dq.shape, jnp.float32)
            for b in range(blocks):
                rows = slice(b * TILE, (b + 1) * TILE)
                for h in range(heads):
                    g = g_ref[rows, h * HD : (h + 1) * HD]
                    split[h, rows, :] = g
                    dots = jnp.sum(g.astype(jnp.float32) * o_ref[h, rows, :], axis=1, keepdims=True)
                    dots = jnp.transpose(jnp.broadcast_to(dots, (TILE, half)))
                    inner[h, :, rows] = dots[0:1, :]

        dk[...] = jnp.zeros(dk.shape, jnp.float32)
        dv[...] = jnp.zeros(dv.shape, jnp.float32)

        def step(i, carry):
            at = pl.ds(pl.multiple_of(i * TILE, TILE), TILE)
            same = twice(col_ref[...]) == row_ref[:, at]
            for h in range(heads):
                q, g, k = q_ref[h, at, :], split[h, at, :], k_ref[h, here, :]
                s = jnp.where(same, nt_dot(k, q), NEG)
                p = jnp.exp(s - lse_ref[h, :, at])
                dp = nt_dot(v_ref[h, here, :], g)
                ds = (p * (dp - inner[h, :, at])).astype(jnp.bfloat16)
                dv[h] = dv[h] + nn_dot(p.astype(jnp.bfloat16), g)
                dk[h] = dk[h] + nn_dot(ds, q)
                dq[h, at, :] = dq[h, at, :] + tn_dot(ds, k)
            return carry

        lax.fori_loop(lo, hi, step, 0)
        cosine, sine = c_ref[here, :], s_ref[here, :]
        for h in range(heads):
            w = dk[h]
            w = (w * cosine - swap_halves(w) * sine).astype(jnp.bfloat16)
            d_ref[here, cols + h * HD : cols + (h + 1) * HD] = w
            d_ref[here, 2 * cols + h * HD : 2 * cols + (h + 1) * HD] = dv[h].astype(jnp.bfloat16)

        @pl.when(j == blocks - 1)
        def _():
            for b in range(blocks):
                rows = slice(b * TILE, (b + 1) * TILE)
                for h in range(heads):
                    w = dq[h, rows, :] * HD**-0.5
                    w = w * c_ref[rows, :] - swap_halves(w) * s_ref[rows, :]
                    d_ref[rows, h * HD : (h + 1) * HD] = w.astype(jnp.bfloat16)

    return pl.pallas_call(
        body,
        grid_spec=pltpu.PrefetchScalarGridSpec(
            num_scalar_prefetch=2,
            grid=(blocks,),
            in_specs=[
                whole(query.shape),
                whole(key.shape),
                whole(value.shape),
                pl.BlockSpec((TILE, half), lambda i, *_: (i, 0)),
                whole(seg_row.shape),
                whole(grad.shape),
                whole(out.shape),
                whole(lse.shape),
                whole(cos_tab.shape),
                whole(sin_tab.shape),
            ],
            out_specs=whole((tok_count, 3 * cols)),
            scratch_shapes=[
                pltpu.VMEM((heads, tok_count, HD), jnp.bfloat16),
                pltpu.VMEM((heads, 1, tok_count), jnp.float32),
                pltpu.VMEM((heads, tok_count, HD), jnp.float32),
                pltpu.VMEM((heads, TILE, HD), jnp.float32),
                pltpu.VMEM((heads, TILE, HD), jnp.float32),
            ],
        ),
        out_shape=jax.ShapeDtypeStruct((tok_count, 3 * cols), jnp.bfloat16),
        name="attend_grad",
    )(first, last, query, key, value, seg_col, seg_row, grad, out, lse, cos_tab, sin_tab)


def shards(
    tokens, lengths, attn_gain, qkv_weight, out_weight, mlp_gain, up_weight, down_weight, cotangent
):
    tok_count = tokens.shape[0]
    qkv_full, up_full = (
        lax.all_gather(qkv_weight, "dp", axis=0, tiled=True),
        lax.all_gather(up_weight, "dp", axis=0, tiled=True),
    )
    out_full, down_full = (
        lax.all_gather(out_weight, "dp", axis=1, tiled=True),
        lax.all_gather(down_weight, "dp", axis=1, tiled=True),
    )
    head_cols = qkv_full.shape[2]
    heads_dev = head_cols // HD
    segment, position = row_layout(lengths[0], tok_count)
    cosine, sine_table = rotary_tables(position, HD)
    source = tokens.astype(jnp.float32)
    normed_one, factor_one = normalize(source)
    h_one = (normed_one * attn_gain).astype(jnp.bfloat16)
    seg_col = jnp.broadcast_to(segment[:, None], (tok_count, TILE // 2))
    seg_row = segment[None, :]
    first, last = tile_ranges(lengths[0], tok_count)
    qkv_flat = qkv_full.reshape(qkv_full.shape[0], 3 * head_cols)
    query, key, value = project_heads(h_one, qkv_flat, cosine, sine_table, heads_dev)
    attended, attended_wide, log_total = attend(first, last, query, key, value, seg_col, seg_row)
    attn_part = jnp.dot(attended, out_full, preferred_element_type=jnp.float32)
    mid = source + lax.psum(attn_part.astype(jnp.bfloat16), "tensor").astype(jnp.float32)
    normed_two, factor_two = normalize(mid)
    h_two = (normed_two * mlp_gain).astype(jnp.bfloat16)
    gate_up = jnp.einsum("td,dcf->tcf", h_two, up_full, preferred_element_type=jnp.float32)
    active, gelu_pull = jax.vjp(exact_gelu, gate_up[:, 0])
    hidden = (active * gate_up[:, 1]).astype(jnp.bfloat16)
    mlp_part = jnp.dot(hidden, down_full, preferred_element_type=jnp.float32)
    output = (mid + lax.psum(mlp_part.astype(jnp.bfloat16), "tensor").astype(jnp.float32)).astype(
        jnp.bfloat16
    )
    grad_down_weight = jnp.einsum(
        "tf,td->fd", hidden, cotangent, preferred_element_type=jnp.float32
    )
    grad_hidden = jnp.einsum(
        "td,fd->tf", cotangent, down_full, preferred_element_type=jnp.float32
    ).astype(jnp.bfloat16)
    grad_wide = grad_hidden.astype(jnp.float32)
    (grad_gate,) = gelu_pull(grad_wide * gate_up[:, 1])
    grad_gate_up = jnp.stack([grad_gate, grad_wide * active], axis=1).astype(jnp.bfloat16)
    grad_up_weight = jnp.einsum(
        "td,tcf->dcf", h_two, grad_gate_up, preferred_element_type=jnp.float32
    )
    grad_h_two = lax.psum(
        jnp.einsum("tcf,dcf->td", grad_gate_up, up_full, preferred_element_type=jnp.float32).astype(
            jnp.bfloat16
        ),
        "tensor",
    ).astype(jnp.float32)
    grad_mlp_gain = jnp.sum(grad_h_two * normed_two, axis=0)
    grad_mid = cotangent.astype(jnp.float32) + norm_back(
        grad_h_two, normed_two, factor_two, mlp_gain
    )
    grad_mid_low = grad_mid.astype(jnp.bfloat16)
    grad_out_weight = jnp.einsum(
        "tf,td->fd", attended, grad_mid_low, preferred_element_type=jnp.float32
    )
    grad_attended = jnp.einsum(
        "td,fd->tf", grad_mid_low, out_full, preferred_element_type=jnp.float32
    ).astype(jnp.bfloat16)
    grad_qkv = attend_grad(
        first,
        last,
        query,
        key,
        value,
        seg_col,
        seg_row,
        grad_attended,
        attended_wide,
        log_total,
        cosine,
        sine_table,
    )
    grad_qkv_weight = jnp.einsum(
        "td,tf->df", h_one, grad_qkv, preferred_element_type=jnp.float32
    ).reshape(-1, 3, head_cols)
    grad_h_one = lax.psum(
        jnp.einsum("tf,df->td", grad_qkv, qkv_flat, preferred_element_type=jnp.float32).astype(
            jnp.bfloat16
        ),
        "tensor",
    ).astype(jnp.float32)
    grad_attn_gain = jnp.sum(grad_h_one * normed_one, axis=0)
    grad_tokens = grad_mid + norm_back(grad_h_one, normed_one, factor_one, attn_gain)
    rows_part = in_one_piece(
        (
            grad_qkv_weight.astype(jnp.bfloat16),
            grad_up_weight.astype(jnp.bfloat16),
            grad_attn_gain.astype(jnp.bfloat16),
            grad_mlp_gain.astype(jnp.bfloat16),
        ),
        "dp",
        0,
        1,
    )
    cols_part = in_one_piece_2(
        (grad_out_weight.astype(jnp.bfloat16), grad_down_weight.astype(jnp.bfloat16)), "dp", 1, 0
    )
    return (
        output,
        grad_tokens,
        rows_part[2],
        rows_part[0],
        cols_part[0],
        rows_part[3],
        rows_part[1],
        cols_part[1],
    )


def solution(mesh):
    in_specs = (
        P("dp", None),
        P("dp", None),
        P(),
        P("dp", None, "tensor"),
        P("tensor", "dp"),
        P(),
        P("dp", None, "tensor"),
        P("tensor", "dp"),
        P("dp", None),
    )
    out_specs = (
        P("dp", None),
        P("dp", None),
        P("dp"),
        P("dp", None, "tensor"),
        P("tensor", "dp"),
        P("dp"),
        P("dp", None, "tensor"),
        P("tensor", "dp"),
    )
    return jax.shard_map(shards, mesh=mesh, in_specs=in_specs, out_specs=out_specs, check_vma=False)
```

time: 871 us -> 590 us (0.68)
  matrix products: 194 us -> 47.8 us
  blocking collectives: 273 us -> 139 us
  Pallas kernels: 0 us -> 88.5 us
  other arithmetic: 131 us -> 61.2 us
  local copies, waits for them, and re-layouts: 98.1 us -> 39.5 us
  waiting for transfers between devices: 141 us -> 166 us
  starting transfers between devices: 11 us -> 22.1 us
    dot_general x32 -> x5, matrix products: 165 us -> 22.4 us  [the longest x1 6.28 us: shards(): jnp.einsum('tf,df->td', grad_qkv, qkv_flat, preferred_element_type=jnp.fl...]
    all_gather x4 -> x0, blocking collectives: 133 us -> none  [the longest x1 35.4 us: shards(): lax.all_gather(held_back[0], 'dp', axis=0, tiled=True)]
    pallas_call x0 -> x3, Pallas kernels: none -> 88.5 us  [the longest x1 53.5 us: attend_grad(): pl.pallas_call(body, grid_spec=pltpu.PrefetchScalarGridSpec(num_scalar_pr...]
    convert_element_type x9 -> x1, other arithmetic: 40 us -> 2.92 us  [shards(): h_one = (normed_one * attn_gain).astype(jnp.bfloat16)]
    dynamic_update_slice x8 -> x0, local copies, waits for them, and re-layouts: 36.1 us -> none  [shards(): attended, log_totals = lax.map(forward_block, (query_blocks, seg_blocks))]
    reduce_sum x5 -> x1, other arithmetic: 28.1 us -> 1.37 us  [row_layout(): segment = jnp.sum(passed.astype(jnp.int32), axis=1, dtype=jnp.int32)]
    psum x2 -> x1, waiting for transfers between devices: 36.6 us -> 52.1 us  [shards(): lax.psum(jnp.einsum('tcf,dcf->td', grad_gate_up, up_full, preferred_eleme...]
    psum x1, waiting for transfers between devices: 68.3 us -> 83.2 us  [shards(): lax.psum(mlp_part.astype(jnp.bfloat16), 'tensor').astype(jnp.float32)]
  transfers between devices with their start and end apart: 6 -> 5, of which waited for: 3 -> 3; matrix products, arithmetic and copies ran while one was open for 6% -> 12% of each run, Pallas kernels for 0% -> 0%
where the time goes in v1:
time: 590 us; the launch traced here: 579 us
  waiting for transfers between devices  166 us (28%)
  blocking collectives  139 us (24%)
  Pallas kernels  88.5 us (15%)
  other arithmetic  61.2 us (10%)
  matrix products  47.8 us (8%)
  local copies, waits for them, and re-layouts  39.5 us (7%)
  starting transfers between devices  22.1 us (4%)
  between operations  14.6 us (2%)
    psum x1, waiting for transfers between devices, shards(): lax.psum(mlp_part.astype(jnp.bfloat16), 'tensor').astype(jnp.float32)  83.2 us
    pallas_call x1, Pallas kernels, attend_grad(): pl.pallas_call(body, grid_spec=pltpu.PrefetchScalarGridSpec(num_scalar_pr...  53.5 us
    psum x1, waiting for transfers between devices, shards(): lax.psum(jnp.einsum('tcf,dcf->td', grad_gate_up, up_full, preferred_eleme...  52.1 us
    all_gather x1, blocking collectives, shards(): lax.all_gather(qkv_weight, 'dp', axis=0, tiled=True)  40.5 us
    all_gather x1, blocking collectives, shards(): lax.all_gather(up_weight, 'dp', axis=0, tiled=True)  34.9 us
    all_gather x1, blocking collectives, shards(): lax.all_gather(down_weight, 'dp', axis=1, tiled=True)  32.2 us
    all_gather x1, blocking collectives, shards(): lax.all_gather(out_weight, 'dp', axis=1, tiled=True)  31.2 us
    all_to_all x2, waiting for transfers between devices, sent_and_summed(): lax.all_to_all(pieces, axis, split_axis=0, concat_axis=0, tiled=True)  31.1 us
  transfers between devices with their start and end apart: 5, of which 3 were waited for; matrix products, arithmetic and copies ran while one was open for 12% of the time, Pallas kernels for 0%

profile of v1, /device:TPU:0, one launch (start us, length us, event | category | flops | bytes accessed | tf_op | source)
XLA Modules:
  0.0 578.8 jit_solution(10133371316329171586)
XLA Ops:
  16.6 40.5 %all_gather.12 = bf16[768,3,192]{2,1,0:T(4,128)(2,1)} all-gather(bf16[96,3,192]{2,1,0:T(4,128)(2,1)S(1)} %copy.102), channel_id=1, replica_groups=mesh['dp'=8,'tensor'=4] {'dp'}, dimensions={0}, use_global_device_ids=true | all-gather | bytes 995328 | tf_op jit(solution)/shard_map/all_gather | solution.py:337
  57.1 3.4 copy.103
  63.4 31.2 %all_gather.13 = bf16[192,768]{0,1:T(8,128)(2,1)S(1)} all-gather(bf16[192,96]{0,1:T(8,128)(2,1)} %copy.106), channel_id=1, replica_groups=mesh['dp'=8,'tensor'=4] {'dp'}, dimensions={1}, use_global_device_ids=true | all-gather | bytes 331776 | tf_op jit(solution)/shard_map/all_gather | solution.py:341
  94.6 4.4 fusion.60
  104.7 8.2 %project_heads.1 = (bf16[3,2048,64]{2,1,0:T(8,128)(2,1)}, bf16[3,2048,64]{2,1,0:T(8,128)(2,1)}, bf16[3,2048,64]{2,1,0:T(8,128)(2,1)}) custom-call(bf16[2048,768]{1,0:T(8,128)(2,1)} %fusion.10.h_ref, bf16[768,576]{1,0:T(8,128)(2,1)} %copy.105.w_ref, f32[2048,64]{1,0:T(8,128)} %get-tuple-element.95.c_ref, f32[2048,64]{1,0:T(8,128)} %get-tuple-element.96.s_ref), custom_call_target="tpu_custom_call" | custom-call | tf_op jit(solution)/shard_map/project_heads/pallas_call | solution.py:145
  114.9 26.9 %attend.1 = (bf16[2048,192]{1,0:T(8,128)(2,1)}, f32[3,2048,64]{2,1,0:T(8,128)}, f32[3,1,2048]{2,1,0:T(1,128)}) custom-call(s32[8]{0:T(128)} %get-tuple-element.94.first_ref, s32[8]{0:T(128)} %get-tuple-element.93.last_ref, bf16[3,2048,64]{2,1,0:T(8,128)(2,1)} %get-tuple-element.14.q_ref, bf16[3,2048,64]{2,1,0:T(8,128)(2,1)} %get-tuple-element.15.k_ref, ...), custom_call_target="tpu_custom_call" | custom-call | tf_op jit(solution)/shard_map/attend/pallas_call | solution.py:206
  141.8 3.9 convolution_convert_fusion.2
  147.4 32.2 %all_gather.15 = bf16[288,768]{0,1:T(8,128)(2,1)S(1)} all-gather(bf16[288,96]{0,1:T(8,128)(2,1)} %copy.108), channel_id=1, replica_groups=mesh['dp'=8,'tensor'=4] {'dp'}, dimensions={1}, use_global_device_ids=true | all-gather | bytes 497664 | tf_op jit(solution)/shard_map/all_gather | solution.py:342
  180.4 4.1 convolution_convert_fusion.3
  184.5 34.9 %all_gather.14 = bf16[768,2,288]{2,1,0:T(2,128)(2,1)} all-gather(bf16[96,2,288]{2,1,0:T(2,128)(2,1)S(1)} %copy-done.13), channel_id=1, replica_groups=mesh['dp'=8,'tensor'=4] {'dp'}, dimensions={0}, use_global_device_ids=true | all-gather | bytes 995328 | tf_op jit(solution)/shard_map/all_gather | solution.py:338
  219.4 2.9 fusion.22
  227.4 5.7 fusion.54
  236.2 4.2 bitcast_convert_fusion
  240.4 10.9 %all-reduce.9.cloned.1.call-start = ((), (), s32[]{:S(2)}) async-start(), calls=%async_computation.4 | async-start | bytes 12582912 | tf_op jit(solution)/shard_map/psum | solution.py:365
  251.4 4.9 convolution_convert_fusion.1
  256.3 52.1 %all-reduce.7.cloned.1.call-done = bf16[2048,768]{1,0:T(8,128)(2,1)} async-done(((bf16[2048,768]{1,0:T(8,128)(2,1)}), bf16[2048,768]{1,0:T(8,128)(2,1)}) %all-reduce.7.cloned.1.call-update) | async-done | bytes 3145744 | tf_op jit(solution)/shard_map/psum | solution.py:380
  308.4 6.8 %fusion.19 = (bf16[768]{0:T(1024)(128)(2,1)}, f32[2048]{0:T(1024)S(1)}, f32[2048]{0:T(1024)S(1)}) fusion(bf16[2048,768]{1,0:T(8,128)(2,1)} %all-reduce.7.cloned.1.call-done, f32[2048]{0:T(1024)} %copy-done.17, f32[2048]{0:T(1024)} %copy-done.14, bf16[2048,768]{1,0:T(8,128)(2,1)} %all-reduce.5.cloned.1.call-done, bf16[2048,768]{1,0:T(8,128)(2,1)S(1)} %copy-done, ...), kind=kLoop, calls=%fused_computation.26 | loop fusion | flops 18869504 | bytes 9474560 | tf_op jit(solution)/shard_map/reduce_sum | solution.py:386
  315.3 3.2 fusion.17
  325.6 53.5 %attend_grad.1 = bf16[2048,576]{1,0:T(8,128)(2,1)} custom-call(s32[8]{0:T(128)} %get-tuple-element.94.first_ref, s32[8]{0:T(128)} %get-tuple-element.93.last_ref, bf16[3,2048,64]{2,1,0:T(8,128)(2,1)} %get-tuple-element.14.q_ref, bf16[3,2048,64]{2,1,0:T(8,128)(2,1)} %get-tuple-element.15.k_ref, bf16[3,2048,64]{2,1,0:T(8,128)(2,1)} %get-tuple-element.16.v_ref, ...), custom_call_target="tpu_custom_call" | custom-call | tf_op jit(solution)/shard_map/attend_grad/pallas_call | solution.py:301
  379.1 6.3 %convolution_convert_fusion = bf16[2048,768]{1,0:T(8,128)(2,1)} fusion(bf16[2048,576]{1,0:T(8,128)(2,1)} %attend_grad.1, bf16[768,576]{0,1:T(8,128)(2,1)} %bitcast.130), kind=kOutput, calls=%fused_computation.37 | convolution fusion | flops 1813512192 | bytes 6389760 | tf_op jit(solution)/shard_map/tf,df->td/dot_general | solution.py:415
  385.4 3.4 convolution_convert_fusion.6
  388.8 4.3 fusion.50
  396.4 5.4 all-to-all-start.1
  401.8 6.1 %fusion.49 = bf16[768,2,288]{0,2,1:T(8,128)(2,1)} fusion(bf16[2048,1,288]{0,2,1:T(8,128)(2,1)} %copy-done.10, bf16[2048,1,288]{0,2,1:T(8,128)(2,1)} %copy-done.8, f32[768]{0:T(1024)S(1)} %copy-done.27, bf16[2048,768]{1,0:T(8,128)(2,1)} %all-reduce.5.cloned.1.call-done, bf16[2048,768]{1,0:T(8,128)(2,1)S(1)} %copy-done, f32[2048]{0:T(1024)S(1)} %copy-done.19, ...), kind=kOutput, calls=%fused_computation.84 | convolution fusion | flops 1828110336 | bytes 9554944 | tf_op jit(solution)/shard_map/td,tcf->dcf/dot_general | solution.py:377
  407.9 3.2 concatenate.20
  413.8 5.7 convolution_convert_fusion.5
  422.1 83.2 %all-reduce.9.cloned.1.call-done = (bf16[2048,768]{1,0:T(8,128)(2,1)}, bf16[2048,768]{1,0:T(8,128)(2,1)}) async-done(((bf16[2048,768]{1,0:T(8,128)(2,1)}, bf16[2048,768]{1,0:T(8,128)(2,1)}), (bf16[2048,768]{1,0:T(8,128)(2,1)}, bf16[2048,768]{1,0:T(8,128)(2,1)})) %all-reduce.9.cloned.1.call-update) | async-done | bytes 6291472 | tf_op jit(solution)/shard_map/psum | solution.py:365
  505.2 5.2 fusion.21
  511.5 4.9 concatenate.21
  516.4 5.7 all-to-all-start
  525.0 11.2 %fusion.13 = (f32[2048,768]{1,0:T(8,128)}, bf16[2048,768]{1,0:T(8,128)(2,1)}) fusion(f32[2048,768]{1,0:T(8,128)} %copy-done.1, bf16[2048,768]{1,0:T(8,128)(2,1)S(1)} %copy-done, bf16[2048,768]{1,0:T(8,128)(2,1)} %get-tuple-element.81, f32[2048]{0:T(1024)S(1)} %broadcast_multiply_fusion, f32[2048]{0:T(1024)S(1)} %broadcast_multiply_fusion.1, ...), kind=kLoop, calls=%fused_computation.20 | loop fusion | flops 23592960 | bytes 28347392 | tf_op jit(solution)/shard_map/add | solution.py:421
  536.1 31.1 %all-to-all-done = bf16[8,96,1154]{2,1,0:T(8,128)(2,1)} async-done(((bf16[8,96,1154]{2,1,0:T(8,128)(2,1)}), bf16[8,96,1154]{2,1,0:T(8,128)(2,1)}, u32[]{:S(2)}, u32[]{:S(2)}) %all-to-all-start) | async-done | bytes 1772576 | tf_op jit(solution)/shard_map/all_to_all | solution.py:25
  (125 shorter events, 54.8 us)
Async XLA Ops:
  7.2 8.2 %copy-start = (bf16[2048,768]{1,0:T(8,128)(2,1)S(1)}, bf16[2048,768]{1,0:T(8,128)(2,1)}, u32[]{:S(2)}) copy-start(bf16[2048,768]{1,0:T(8,128)(2,1)} %param.9) | copy-start | bytes 9437188
  7.2 212.3 %all-reduce.5.cloned.1.call-start = ((), (), s32[]{:S(2)}) async-start(), calls=%async_computation.2 | async-start | bytes 6291456 | tf_op jit(solution)/shard_map/psum | solution.py:358
  9.7 6.7 %copy-start.29 = (s32[16]{0:T(128)}, s32[16]{0:T(128)S(1)}, u32[]{:S(2)}) copy-start(s32[16]{0:T(128)S(1)} %reduce) | copy-start | bytes 196
  12.9 3.5 copy-start.12
  16.4 46.3 %copy-start.20 = (bf16[192,96]{1,0:T(8,128)(2,1)S(1)}, bf16[192,96]{1,0:T(8,128)(2,1)}, u32[]{:S(2)}) copy-start(bf16[192,96]{1,0:T(8,128)(2,1)} %param.13) | copy-start | bytes 110596
  99.0 3.0 copy-start.30
  99.0 3.0 copy-start.31
  99.0 2.9 copy-start.32
  99.1 2.9 copy-start.33
  145.7 162.7 %all-reduce.7.cloned.1.call-start = ((), (), s32[]{:S(2)}) async-start(), calls=%async_computation.3 | async-start | bytes 6291456 | tf_op jit(solution)/shard_map/psum | solution.py:380
  147.4 37.1 %copy-start.13 = (bf16[96,2,288]{2,1,0:T(2,128)(2,1)S(1)}, bf16[96,2,288]{2,1,0:T(2,128)(2,1)}, u32[]{:S(2)}) copy-start(bf16[96,2,288]{2,1,0:T(2,128)(2,1)} %param.15) | copy-start | bytes 331780
  219.4 2.9 copy-start.2
  224.6 2.8 copy-start.5
  240.4 264.8 %all-reduce.9.cloned.1.call-start = ((), (), s32[]{:S(2)}) async-start(), calls=%async_computation.4 | async-start | bytes 12582912 | tf_op jit(solution)/shard_map/psum | solution.py:365
  308.4 6.8 %copy-start.3 = (bf16[2048,768]{1,0:T(8,128)(2,1)S(1)}, bf16[2048,768]{1,0:T(8,128)(2,1)}, u32[]{:S(2)}) copy-start(bf16[2048,768]{1,0:T(8,128)(2,1)} %all-reduce.5.cloned.1.call-done) | copy-start | bytes 9437188
  308.4 6.8 %copy-start.4 = (bf16[2048,768]{1,0:T(8,128)(2,1)S(1)}, bf16[2048,768]{1,0:T(8,128)(2,1)}, u32[]{:S(2)}) copy-start(bf16[2048,768]{1,0:T(8,128)(2,1)} %all-reduce.7.cloned.1.call-done) | copy-start | bytes 9437188
  308.4 6.8 %copy-start.7 = (bf16[2048,768]{1,0:T(8,128)(2,1)S(1)}, bf16[2048,768]{1,0:T(8,128)(2,1)}, u32[]{:S(2)}) copy-start(bf16[2048,768]{1,0:T(8,128)(2,1)} %param.17) | copy-start | bytes 9437188
  308.4 6.8 %copy-start.15 = (f32[2048]{0:T(1024)S(1)}, f32[2048]{0:T(1024)}, u32[]{:S(2)}) copy-start(f32[2048]{0:T(1024)} %copy-done.14) | copy-start | bytes 24580
  308.4 6.8 %copy-start.18 = (f32[2048]{0:T(1024)S(1)}, f32[2048]{0:T(1024)}, u32[]{:S(2)}) copy-start(f32[2048]{0:T(1024)} %copy-done.17) | copy-start | bytes 24580
  308.4 6.8 %copy-start.26 = (f32[768]{0:T(1024)S(1)}, f32[768]{0:T(1024)}, u32[]{:S(2)}) copy-start(f32[768]{0:T(1024)} %param.14) | copy-start | bytes 9220
  318.5 2.7 copy-start.1
  385.4 3.4 copy-start.6
  393.1 8.7 %copy-start.16 = (f32[2048]{0:T(1024)S(1)}, f32[2048]{0:T(1024)}, u32[]{:S(2)}) copy-start(f32[2048]{0:T(1024)} %copy-done.14) | copy-start | bytes 24580
  393.1 8.7 %copy-start.19 = (f32[2048]{0:T(1024)S(1)}, f32[2048]{0:T(1024)}, u32[]{:S(2)}) copy-start(f32[2048]{0:T(1024)} %copy-done.17) | copy-start | bytes 24580
  393.1 8.7 %copy-start.27 = (f32[768]{0:T(1024)S(1)}, f32[768]{0:T(1024)}, u32[]{:S(2)}) copy-start(f32[768]{0:T(1024)} %param.14) | copy-start | bytes 9220
  396.4 120.0 %all-to-all-start.1 = ((bf16[8,480,96]{1,2,0:T(8,128)(2,1)}), bf16[8,480,96]{1,2,0:T(8,128)(2,1)}, u32[]{:S(2)}, u32[]{:S(2)}) async-start(bf16[8,480,96]{1,2,0:T(8,128)(2,1)} %bitcast.131), calls=%async_computation.1 | async-start | bytes 1572864 | tf_op jit(solution)/shard_map/all_to_all | solution.py:25
  413.8 7.9 %copy-start.28 = (bf16[768]{0:T(1024)(128)(2,1)S(1)}, bf16[768]{0:T(1024)(128)(2,1)}, u32[]{:S(2)}) copy-start(bf16[768]{0:T(1024)(128)(2,1)} %get-tuple-element.68) | copy-start | bytes 4612
  413.8 91.4 %copy-start.21 = (f32[768]{0:T(1024)S(1)}, f32[768]{0:T(1024)}, u32[]{:S(2)}) copy-start(f32[768]{0:T(1024)} %param.11) | copy-start | bytes 9220
  516.4 8.6 %copy-start.24 = (f32[2048]{0:T(1024)S(1)}, f32[2048]{0:T(1024)}, u32[]{:S(2)}) copy-start(f32[2048]{0:T(1024)} %get-tuple-element.71) | copy-start | bytes 24580
  516.4 8.6 %copy-start.23 = (f32[2048]{0:T(1024)S(1)}, f32[2048]{0:T(1024)}, u32[]{:S(2)}) copy-start(f32[2048]{0:T(1024)} %get-tuple-element.72) | copy-start | bytes 24580
  516.4 8.6 %copy-start.22 = (f32[768]{0:T(1024)S(1)}, f32[768]{0:T(1024)}, u32[]{:S(2)}) copy-start(f32[768]{0:T(1024)} %param.11) | copy-start | bytes 9220
  516.4 50.8 %all-to-all-start = ((bf16[8,96,1154]{2,1,0:T(8,128)(2,1)}), bf16[8,96,1154]{2,1,0:T(8,128)(2,1)}, u32[]{:S(2)}, u32[]{:S(2)}) async-start(bf16[8,96,1154]{2,1,0:T(8,128)(2,1)} %concatenate.21), calls=%async_computation | async-start | bytes 3932160 | tf_op jit(solution)/shard_map/all_to_all | solution.py:25
  (7 other events, 10.6 us)
Sparse Core Ops, SparseCore 0:
  145.8 67.8 all-reduce.4
  240.6 67.7 all-reduce.6
  385.5 119.6 all-reduce.8
